TPU v7x, 32 devices: a whole 2x2x4 slice. The times are simulated.
32 devices in a mesh: groups: 2 (over y), shots: 4 (over z), dom: 2 (over x), sub: 2 (over core).
Axes of the slice: x: 2, y: 2, z: 4, core: 2. Of those that a mesh axis runs over, the one named last changes fastest.
Arguments:
- velocity: float32 [64, 16, 256], P(('groups', 'shots'), 'dom', 'sub'), parts along dimension 0, may hold values from 0.15 to 0.4
- wave_prev: bfloat16 [8, 32, 16, 256], P(('groups', 'shots'), None, 'dom', 'sub'), parts along dimension 0, may hold values from -6 to 6
- wave_now: bfloat16 [8, 32, 16, 256], P(('groups', 'shots'), None, 'dom', 'sub'), parts along dimension 0, may hold values from -6 to 6
- adj_next: bfloat16 [8, 32, 16, 256], P(('groups', 'shots'), None, 'dom', 'sub'), parts along dimension 0, may hold values from -6 to 6
- adj_now: bfloat16 [8, 32, 16, 256], P(('groups', 'shots'), None, 'dom', 'sub'), parts along dimension 0, may hold values from -6 to 6
- sponge: int32 [32, 16, 256], P(None, 'dom', 'sub'), may hold values 0 or 1
- wavelet: float32 [8, 6], P(('groups', 'shots')), parts along dimension 0, may hold values from -12 to 12
- src_pos: int32 [8], P(('groups', 'shots')), parts along dimension 0, may hold values from 0 to 4095
- rec_pos: int32 [8, 256], P(('groups', 'shots')), parts along dimension 0, may hold values from 0 to 4095
- observed: float32 [8, 4, 256], P(('groups', 'shots')), parts along dimension 0, may hold values from -6 to 6
Outputs:
- direction: float32 [64, 16, 256], P(('groups', 'shots'), 'dom', 'sub'), parts along dimension 0
- wave_out: float32 [8, 32, 16, 256], P(('groups', 'shots'), None, 'dom', 'sub'), parts along dimension 0
There are 2 independent parts, one for each index of `groups`. A program takes and returns all parts, laid end to end along the dimension named above; an argument that names none is the same for every part. Nothing has to cross between parts.
Inputs may be any that keep to these rules, and one draw needn't show every extreme that they name: `src_pos`: a horizontal position x * 256 + y on the grid. `rec_pos`: horizontal positions x * 256 + y on the grid, possibly repeated.
All inputs are finite; a program needn't handle non-finite values. Where the computation divides by a largest or mean magnitude, that divisor is 1e-20 or more. No bound on the sum of `sponge` on one device may be relied on, other than what follows from the above.
Results may differ from a plain program's by a relative error of at most 0.0003.
Values sent between devices are 32-bit elements; how exact they have to be, the bound alone decides.
A program may use at most 64 MiB of HBM per device.

v0:
```python
import jax
import jax.numpy as jnp
from jax import lax
from jax.sharding import PartitionSpec as P

NF = 4
NFIN = 2
coeffs = (-205.0 / 72.0, 8.0 / 5.0, -1.0 / 5.0, 8.0 / 315.0, -1.0 / 560.0)
damp_rate = 0.2
step_rate = 0.1
floor_share = 0.5
src_depth = 2
rec_depth = 1
reach = 4


def padded_2(cells, sides, width):
    for axis, dim in sides:
        count = lax.axis_size(axis)
        ends = count - 1
        head = lax.slice_in_dim(cells, 0, width, axis=dim)
        tail = lax.slice_in_dim(cells, cells.shape[dim] - width, cells.shape[dim], axis=dim)
        cells = jnp.concatenate(
            [
                lax.ppermute(tail, axis, [(i, (i + 1) % count) for i in range(ends)]),
                cells,
                lax.ppermute(head, axis, [((i + 1) % count, i) for i in range(ends)]),
            ],
            axis=dim,
        )
    return cells


def laplace(padded, depth, rows, cols):
    z0, x0, y0 = (reach, reach, reach)
    total = 3.0 * coeffs[0] * padded[z0 : z0 + depth, x0 : x0 + rows, y0 : y0 + cols]
    for offset in range(1, 5):
        pair = padded[z0 + offset : z0 + offset + depth, x0 : x0 + rows, y0 : y0 + cols]
        pair = pair + padded[z0 - offset : z0 - offset + depth, x0 : x0 + rows, y0 : y0 + cols]
        pair = pair + padded[z0 : z0 + depth, x0 + offset : x0 + offset + rows, y0 : y0 + cols]
        pair = pair + padded[z0 : z0 + depth, x0 - offset : x0 - offset + rows, y0 : y0 + cols]
        pair = pair + padded[z0 : z0 + depth, x0 : x0 + rows, y0 + offset : y0 + offset + cols]
        pair = pair + padded[z0 : z0 + depth, x0 : x0 + rows, y0 - offset : y0 - offset + cols]
        total = total + coeffs[offset] * pair
    return total


def advance(now, before, kappa, damp, plane, level):
    widened = padded_2(now, (("dom", 1), ("sub", 2)), 4)
    padded = jnp.pad(widened, ((reach, reach), (0, 0), (0, 0)))
    lap = laplace(padded, now.shape[0], now.shape[1], now.shape[2])
    numer = 2.0 * now - (1.0 - damp) * before + kappa * lap
    numer = numer.at[level].add(plane)
    return numer / (1.0 + damp)


def local_spots(positions, rows, cols):
    cols_all = cols * lax.axis_size("sub")
    gx = positions // cols_all
    gy = positions % cols_all
    local_x = gx - lax.axis_index("dom") * rows
    local_y = gy - lax.axis_index("sub") * cols
    inside = (local_x >= 0) & (local_x < rows) & (local_y >= 0) & (local_y < cols)
    spots = jnp.where(inside, local_x * cols + local_y, 0)
    return (spots, inside)


def place_local(spots, inside, values, rows, cols):
    kept = jnp.where(inside, values, 0.0)
    flat = jnp.zeros((rows * cols,), jnp.float32).at[spots].add(kept)
    return flat.reshape(rows, cols)


def shards(
    velocity, wave_prev, wave_now, adj_next, adj_now, sponge, wavelet, src_pos, rec_pos, observed
):
    depth, rows, cols = sponge.shape
    full_vel = lax.all_gather(velocity, "shots", axis=0, tiled=True)
    kappa = full_vel * full_vel
    damp = damp_rate * sponge.astype(jnp.float32)
    amps = wavelet[0]
    src_spot, src_inside = local_spots(src_pos, rows, cols)
    rec_spot, rec_inside = local_spots(rec_pos[0], rows, cols)
    states = [wave_prev[0].astype(jnp.float32), wave_now[0].astype(jnp.float32)]
    for step in range(NF):
        plane = place_local(src_spot, src_inside, amps[step][None], rows, cols)
        states.append(advance(states[-1], states[-2], kappa, damp, plane, src_depth))
    lam_after = adj_next[0].astype(jnp.float32)
    lam_now = adj_now[0].astype(jnp.float32)
    grad = jnp.zeros_like(kappa)
    for level in range(NF, 0, -1):
        sampled = states[level + 1][rec_depth].reshape(-1)[rec_spot]
        resid = sampled - observed[0, level - 1]
        plane = place_local(rec_spot, rec_inside, resid, rows, cols)
        lam_before = advance(lam_now, lam_after, kappa, damp, plane, rec_depth)
        lower = level - 1
        accel = states[lower + 2] - 2.0 * states[lower + 1] + states[lower]
        grad = grad + lam_before * accel
        lam_after, lam_now = (lam_now, lam_before)
    illum = jnp.zeros_like(kappa)
    for level in range(1, NF + 1):
        illum = illum + states[level + 1] * states[level + 1]
    shot_count = lax.axis_size("shots")
    grad_all, illum_all = lax.psum((grad, illum), "shots")
    precond = grad_all / (illum_all + floor_share * shot_count)
    peak = lax.pmax(jnp.max(jnp.abs(precond)), ("dom", "sub"))
    full_dir = precond / (peak + 1e-06)
    updated = full_vel * (1.0 - step_rate * full_dir)
    owned = velocity.shape[0]
    direction = lax.dynamic_slice_in_dim(full_dir, lax.axis_index("shots") * owned, owned, 0)
    kappa_new = updated * updated
    before, current = (states[-2], states[-1])
    for step in range(NFIN):
        plane = place_local(src_spot, src_inside, amps[NF + step][None], rows, cols)
        following = advance(current, before, kappa_new, damp, plane, src_depth)
        before, current = (current, following)
    return (direction, current[None])


def solution(mesh):
    return jax.shard_map(
        shards,
        mesh=mesh,
        in_specs=(
            P(("groups", "shots"), "dom", "sub"),
            P(("groups", "shots"), None, "dom", "sub"),
            P(("groups", "shots"), None, "dom", "sub"),
            P(("groups", "shots"), None, "dom", "sub"),
            P(("groups", "shots"), None, "dom", "sub"),
            P(None, "dom", "sub"),
            P(("groups", "shots"), None),
            P(("groups", "shots")),
            P(("groups", "shots"), None),
            P(("groups", "shots"), None, None),
        ),
        out_specs=(
            P(("groups", "shots"), "dom", "sub"),
            P(("groups", "shots"), None, "dom", "sub"),
        ),
        check_vma=False,
    )
```

profile of v0, /device:TPU:0, one launch (start us, length us, event | category | flops | bytes accessed | tf_op | source)
XLA Modules:
  0.0 231.8 jit_solution(6835556315163786703)
XLA Ops:
  8.1 4.9 %collective-permute-start.4 = (f32[32,4,128]{2,1,0:T(4,128)S(1)}, f32[32,4,128]{2,1,0:T(4,128)S(1)}, u32[]{:S(2)}, u32[]{:S(2)}) collective-permute-start(f32[32,4,128]{2,1,0:T(4,128)S(1)} %get-tuple-element.261), channel_id=1, source_target_pairs={{0,2},{1,3},{4,6},{5,7},{8,10},{9,11},{12,14},{13,15},{16,18},{17,... | collective-permute-start | bytes 196616 | tf_op jit(solution)/shard_map/ppermute | solution.py:25
  14.3 4.5 %collective-permute-start = (f32[32,4,128]{2,1,0:T(4,128)S(1)}, f32[32,4,128]{2,1,0:T(4,128)S(1)}, u32[]{:S(2)}, u32[]{:S(2)}) collective-permute-start(f32[32,4,128]{2,1,0:T(4,128)S(1)} %get-tuple-element.251), channel_id=1, source_target_pairs={{0,2},{1,3},{4,6},{5,7},{8,10},{9,11},{12,14},{13,15},{16,18},{17,... | collective-permute-start | bytes 196616 | tf_op jit(solution)/shard_map/ppermute | solution.py:25
  27.0 2.6 %fusion.344 = f32[1024]{0:T(1024)S(1)} fusion(f32[1024]{0:T(1024)S(1)} %broadcast.395.clone, s32[]{:T(128)} %bitcast.12, pred[1]{0:T(512)(128)(4,1)} %get-tuple-element.275, f32[1,1]{1,0:T(1,128)} %get-tuple-element.270, s32[1]{0:T(128)} %compare_select_fusion.1), kind=kLoop, calls=%fused_computation.685 | loop fusion | flops 5 | bytes 525 | tf_op jit(solution)/shard_map/scatter-add | solution.py:70
  29.6 2.6 %fusion.342 = f32[1024]{0:T(1024)S(1)} fusion(f32[1024]{0:T(1024)S(1)} %broadcast.395.clone.1, s32[]{:T(128)} %bitcast.12, pred[1]{0:T(512)(128)(4,1)} %get-tuple-element.275, f32[1,1]{1,0:T(1,128)} %get-tuple-element.269, s32[1]{0:T(128)} %compare_select_fusion.1), kind=kLoop, calls=%fused_computation.682 | loop fusion | flops 5 | bytes 525 | tf_op jit(solution)/shard_map/scatter-add | solution.py:70
  32.3 2.6 %fusion.340 = f32[1024]{0:T(1024)S(1)} fusion(f32[1024]{0:T(1024)S(1)} %broadcast.395.clone.2, s32[]{:T(128)} %bitcast.12, pred[1]{0:T(512)(128)(4,1)} %get-tuple-element.275, f32[1,1]{1,0:T(1,128)} %get-tuple-element.268, s32[1]{0:T(128)} %compare_select_fusion.1), kind=kLoop, calls=%fused_computation.679 | loop fusion | flops 5 | bytes 525 | tf_op jit(solution)/shard_map/scatter-add | solution.py:70
  34.9 2.6 %fusion.338 = f32[1024]{0:T(1024)S(1)} fusion(f32[1024]{0:T(1024)S(1)} %broadcast.395.clone.3, s32[]{:T(128)} %bitcast.12, pred[1]{0:T(512)(128)(4,1)} %get-tuple-element.275, f32[1,1]{1,0:T(1,128)} %get-tuple-element.267, s32[1]{0:T(128)} %compare_select_fusion.1), kind=kLoop, calls=%fused_computation.676 | loop fusion | flops 5 | bytes 525 | tf_op jit(solution)/shard_map/scatter-add | solution.py:70
  37.5 13.6 %all_gather.3 = f32[32,8,128]{2,1,0:T(8,128)S(1)} all-gather(f32[8,8,128]{2,1,0:T(8,128)S(1)} %copy-done.7), channel_id=1, replica_groups=mesh['groups'=2,'shots'=4,'dom'=2,'sub'=2] {'shots'}, dimensions={0}, use_global_device_ids=true | all-gather | bytes 163840 | tf_op jit(solution)/shard_map/all_gather | solution.py:78
  54.1 3.1 %collective-permute-start.2 = (f32[32,16,4]{2,1,0:T(8,128)S(1)}, f32[32,16,4]{2,1,0:T(8,128)S(1)}, u32[]{:S(2)}, u32[]{:S(2)}) collective-permute-start(f32[32,16,4]{2,1,0:T(8,128)S(1)} %get-tuple-element.221), channel_id=1, source_target_pairs={{0,1},{2,3},{4,5},{6,7},{8,9},{10,11},{12,13},{14,15},{16,17},{18,... | collective-permute-start | bytes 24584 | tf_op jit(solution)/shard_map/ppermute | solution.py:25
  60.5 4.5 %collective-permute-start.8 = (f32[32,4,128]{2,1,0:T(4,128)S(1)}, f32[32,4,128]{2,1,0:T(4,128)S(1)}, u32[]{:S(2)}, u32[]{:S(2)}) collective-permute-start(f32[32,4,128]{2,1,0:T(4,128)S(1)} %get-tuple-element.259), channel_id=1, source_target_pairs={{0,2},{1,3},{4,6},{5,7},{8,10},{9,11},{12,14},{13,15},{16,18},{17,... | collective-permute-start | bytes 196616 | tf_op jit(solution)/shard_map/ppermute | solution.py:25
  67.3 4.5 %collective-permute-done.9 = f32[32,4,128]{2,1,0:T(4,128)S(1)} collective-permute-done((f32[32,4,128]{2,1,0:T(4,128)S(1)}, f32[32,4,128]{2,1,0:T(4,128)S(1)}, u32[]{:S(2)}, u32[]{:S(2)}) %collective-permute-start.9) | collective-permute-done | bytes 65568 | tf_op jit(solution)/shard_map/ppermute | solution.py:27
  83.0 3.5 %collective-permute-done.13 = f32[32,4,128]{2,1,0:T(4,128)S(1)} collective-permute-done((f32[32,4,128]{2,1,0:T(4,128)S(1)}, f32[32,4,128]{2,1,0:T(4,128)S(1)}, u32[]{:S(2)}, u32[]{:S(2)}) %collective-permute-start.13) | collective-permute-done | bytes 65568 | tf_op jit(solution)/shard_map/ppermute | solution.py:27
  97.1 3.5 %collective-permute-done.17 = f32[32,4,128]{2,1,0:T(4,128)S(1)} collective-permute-done((f32[32,4,128]{2,1,0:T(4,128)S(1)}, f32[32,4,128]{2,1,0:T(4,128)S(1)}, u32[]{:S(2)}, u32[]{:S(2)}) %collective-permute-start.17) | collective-permute-done | bytes 65568 | tf_op jit(solution)/shard_map/ppermute | solution.py:27
  109.0 2.3 %scatter_custom_fusion = f32[1024]{0:T(1024)S(1)} fusion(s32[256]{0:T(256)S(1)} %bitcast.109, f32[256]{0:T(256)S(1)} %get-tuple-element.274, f32[]{:T(128)} %constant.405.clone.1), kind=kCustom, calls=%fused_computation.646 | custom fusion | flops 256 | bytes 4100 | tf_op jit(solution)/shard_map/scatter-add | solution.py:70
  115.1 4.1 %collective-permute-done.21 = f32[32,4,128]{2,1,0:T(4,128)S(1)} collective-permute-done((f32[32,4,128]{2,1,0:T(4,128)S(1)}, f32[32,4,128]{2,1,0:T(4,128)S(1)}, u32[]{:S(2)}, u32[]{:S(2)}) %collective-permute-start.21) | collective-permute-done | bytes 65568 | tf_op jit(solution)/shard_map/ppermute | solution.py:27
  122.1 2.3 %scatter_custom_fusion.1 = f32[1024]{0:T(1024)S(1)} fusion(s32[256]{0:T(256)S(1)} %bitcast.110, f32[256]{0:T(256)S(1)} %get-tuple-element.273, f32[]{:T(128)} %constant.405.clone.1), kind=kCustom, calls=%fused_computation.644 | custom fusion | flops 256 | bytes 4100 | tf_op jit(solution)/shard_map/scatter-add | solution.py:70
  129.7 4.5 %collective-permute-done.25 = f32[32,4,128]{2,1,0:T(4,128)S(1)} collective-permute-done((f32[32,4,128]{2,1,0:T(4,128)S(1)}, f32[32,4,128]{2,1,0:T(4,128)S(1)}, u32[]{:S(2)}, u32[]{:S(2)}) %collective-permute-start.25) | collective-permute-done | bytes 65568 | tf_op jit(solution)/shard_map/ppermute | solution.py:27
  140.0 2.3 %scatter_custom_fusion.2 = f32[1024]{0:T(1024)S(1)} fusion(s32[256]{0:T(256)S(1)} %bitcast.112, f32[256]{0:T(256)S(1)} %get-tuple-element.272, f32[]{:T(128)} %constant.405.clone.1), kind=kCustom, calls=%fused_computation.642 | custom fusion | flops 256 | bytes 4100 | tf_op jit(solution)/shard_map/scatter-add | solution.py:70
  146.6 4.5 %collective-permute-start.32 = (f32[32,4,128]{2,1,0:T(4,128)S(1)}, f32[32,4,128]{2,1,0:T(4,128)S(1)}, u32[]{:S(2)}, u32[]{:S(2)}) collective-permute-start(f32[32,4,128]{2,1,0:T(4,128)S(1)} %get-tuple-element.253), channel_id=1, source_target_pairs={{0,2},{1,3},{4,6},{5,7},{8,10},{9,11},{12,14},{13,15},{16,18},{17,... | collective-permute-start | bytes 196616 | tf_op jit(solution)/shard_map/ppermute | solution.py:25
  152.7 2.3 %collective-permute-start.30 = (f32[32,16,4]{2,1,0:T(8,128)S(1)}, f32[32,16,4]{2,1,0:T(8,128)S(1)}, u32[]{:S(2)}, u32[]{:S(2)}) collective-permute-start(f32[32,16,4]{2,1,0:T(8,128)S(1)} %get-tuple-element.209), channel_id=1, source_target_pairs={{0,1},{2,3},{4,5},{6,7},{8,9},{10,11},{12,13},{14,15},{16,17},{18,... | collective-permute-start | bytes 24584 | tf_op jit(solution)/shard_map/ppermute | solution.py:25
  164.2 2.6 %fusion.336 = f32[1024]{0:T(1024)S(1)} fusion(f32[1024]{0:T(1024)S(1)} %broadcast.395.clone.4, s32[]{:T(128)} %bitcast.12, pred[1]{0:T(512)(128)(4,1)} %get-tuple-element.275, f32[1,1]{1,0:T(1,128)} %get-tuple-element.271, s32[1]{0:T(128)} %compare_select_fusion.1), kind=kLoop, calls=%fused_computation.673 | loop fusion | flops 5 | bytes 525 | tf_op jit(solution)/shard_map/scatter-add | solution.py:70
  167.1 31.3 %all-reduce.13.cloned.1.call-done = (f32[32,8,128]{2,1,0:T(8,128)}, f32[32,8,128]{2,1,0:T(8,128)}) async-done(((f32[32,8,128]{2,1,0:T(8,128)}, f32[32,8,128]{2,1,0:T(8,128)}), (f32[32,8,128]{2,1,0:T(8,128)}, f32[32,8,128]{2,1,0:T(8,128)})) %all-reduce.13.cloned.1.call-update) | async-done | bytes 262160 | tf_op jit(solution)/shard_map/psum | solution.py:104
  200.4 6.3 %pmax.7 = f32[]{:T(128)} all-reduce(f32[]{:T(128)} %abs_reduce_fusion), channel_id=1, replica_groups=mesh['groups'=2,'shots'=4,'dom'=2,'sub'=2] {'dom','sub'}, use_global_device_ids=true, to_apply=%region_7.8 | all-reduce | flops 1 | bytes 8 | tf_op jit(solution)/shard_map/pmax | solution.py:106
  208.1 3.6 %collective-permute-start.36 = (f32[32,4,128]{2,1,0:T(4,128)S(1)}, f32[32,4,128]{2,1,0:T(4,128)S(1)}, u32[]{:S(2)}, u32[]{:S(2)}) collective-permute-start(f32[32,4,128]{2,1,0:T(4,128)S(1)} %get-tuple-element.243), channel_id=1, source_target_pairs={{0,2},{1,3},{4,6},{5,7},{8,10},{9,11},{12,14},{13,15},{16,18},{17,... | collective-permute-start | bytes 196616 | tf_op jit(solution)/shard_map/ppermute | solution.py:25
  213.1 2.6 %fusion.334 = f32[1024]{0:T(1024)S(1)} fusion(f32[1024]{0:T(1024)S(1)} %broadcast.395.clone.5, s32[]{:T(128)} %bitcast.12, pred[1]{0:T(512)(128)(4,1)} %get-tuple-element.275, f32[1,1]{1,0:T(1,128)} %get-tuple-element.266, s32[1]{0:T(128)} %compare_select_fusion.1), kind=kLoop, calls=%fused_computation.670 | loop fusion | flops 5 | bytes 525 | tf_op jit(solution)/shard_map/scatter-add | solution.py:70
  (198 shorter events, 90.9 us)
Async XLA Ops:
  7.2 191.2 %all-reduce.13.cloned.1.call-start = ((), (), s32[]{:S(2)}) async-start(), calls=%async_computation | async-start | bytes 524288 | tf_op jit(solution)/shard_map/psum | solution.py:104
  8.1 43.0 %collective-permute-start.4 = (f32[32,4,128]{2,1,0:T(4,128)S(1)}, f32[32,4,128]{2,1,0:T(4,128)S(1)}, u32[]{:S(2)}, u32[]{:S(2)}) collective-permute-start(f32[32,4,128]{2,1,0:T(4,128)S(1)} %get-tuple-element.261), channel_id=1, source_target_pairs={{0,2},{1,3},{4,6},{5,7},{8,10},{9,11},{12,14},{13,15},{16,18},{17,... | collective-permute-start | bytes 196616 | tf_op jit(solution)/shard_map/ppermute | solution.py:25
  13.0 38.1 %collective-permute-start.5 = (f32[32,4,128]{2,1,0:T(4,128)S(1)}, f32[32,4,128]{2,1,0:T(4,128)S(1)}, u32[]{:S(2)}, u32[]{:S(2)}) collective-permute-start(f32[32,4,128]{2,1,0:T(4,128)S(1)} %get-tuple-element.260), channel_id=1, source_target_pairs={{2,0},{3,1},{6,4},{7,5},{10,8},{11,9},{14,12},{15,13},{18,16},{19,... | collective-permute-start | bytes 196616 | tf_op jit(solution)/shard_map/ppermute | solution.py:27
  14.3 39.5 %collective-permute-start = (f32[32,4,128]{2,1,0:T(4,128)S(1)}, f32[32,4,128]{2,1,0:T(4,128)S(1)}, u32[]{:S(2)}, u32[]{:S(2)}) collective-permute-start(f32[32,4,128]{2,1,0:T(4,128)S(1)} %get-tuple-element.251), channel_id=1, source_target_pairs={{0,2},{1,3},{4,6},{5,7},{8,10},{9,11},{12,14},{13,15},{16,18},{17,... | collective-permute-start | bytes 196616 | tf_op jit(solution)/shard_map/ppermute | solution.py:25
  18.9 35.0 %collective-permute-start.1 = (f32[32,4,128]{2,1,0:T(4,128)S(1)}, f32[32,4,128]{2,1,0:T(4,128)S(1)}, u32[]{:S(2)}, u32[]{:S(2)}) collective-permute-start(f32[32,4,128]{2,1,0:T(4,128)S(1)} %get-tuple-element.250), channel_id=1, source_target_pairs={{2,0},{3,1},{6,4},{7,5},{10,8},{11,9},{14,12},{15,13},{18,16},{19,... | collective-permute-start | bytes 196616 | tf_op jit(solution)/shard_map/ppermute | solution.py:27
  51.3 7.2 %collective-permute-start.6 = (f32[32,16,4]{2,1,0:T(8,128)S(1)}, f32[32,16,4]{2,1,0:T(8,128)S(1)}, u32[]{:S(2)}, u32[]{:S(2)}) collective-permute-start(f32[32,16,4]{2,1,0:T(8,128)S(1)} %get-tuple-element.241), channel_id=1, source_target_pairs={{0,1},{2,3},{4,5},{6,7},{8,9},{10,11},{12,13},{14,15},{16,17},{18,... | collective-permute-start | bytes 24584 | tf_op jit(solution)/shard_map/ppermute | solution.py:25
  52.6 5.9 %collective-permute-start.7 = (f32[32,16,4]{2,1,0:T(8,128)S(1)}, f32[32,16,4]{2,1,0:T(8,128)S(1)}, u32[]{:S(2)}, u32[]{:S(2)}) collective-permute-start(f32[32,16,4]{2,1,0:T(8,128)S(1)} %get-tuple-element.240), channel_id=1, source_target_pairs={{1,0},{3,2},{5,4},{7,6},{9,8},{11,10},{13,12},{15,14},{17,16},{19,... | collective-permute-start | bytes 24584 | tf_op jit(solution)/shard_map/ppermute | solution.py:27
  54.1 12.2 %collective-permute-start.2 = (f32[32,16,4]{2,1,0:T(8,128)S(1)}, f32[32,16,4]{2,1,0:T(8,128)S(1)}, u32[]{:S(2)}, u32[]{:S(2)}) collective-permute-start(f32[32,16,4]{2,1,0:T(8,128)S(1)} %get-tuple-element.221), channel_id=1, source_target_pairs={{0,1},{2,3},{4,5},{6,7},{8,9},{10,11},{12,13},{14,15},{16,17},{18,... | collective-permute-start | bytes 24584 | tf_op jit(solution)/shard_map/ppermute | solution.py:25
  57.2 9.2 %collective-permute-start.3 = (f32[32,16,4]{2,1,0:T(8,128)S(1)}, f32[32,16,4]{2,1,0:T(8,128)S(1)}, u32[]{:S(2)}, u32[]{:S(2)}) collective-permute-start(f32[32,16,4]{2,1,0:T(8,128)S(1)} %get-tuple-element.220), channel_id=1, source_target_pairs={{1,0},{3,2},{5,4},{7,6},{9,8},{11,10},{13,12},{15,14},{17,16},{19,... | collective-permute-start | bytes 24584 | tf_op jit(solution)/shard_map/ppermute | solution.py:27
  60.5 6.9 %collective-permute-start.8 = (f32[32,4,128]{2,1,0:T(4,128)S(1)}, f32[32,4,128]{2,1,0:T(4,128)S(1)}, u32[]{:S(2)}, u32[]{:S(2)}) collective-permute-start(f32[32,4,128]{2,1,0:T(4,128)S(1)} %get-tuple-element.259), channel_id=1, source_target_pairs={{0,2},{1,3},{4,6},{5,7},{8,10},{9,11},{12,14},{13,15},{16,18},{17,... | collective-permute-start | bytes 196616 | tf_op jit(solution)/shard_map/ppermute | solution.py:25
  65.0 6.7 %collective-permute-start.9 = (f32[32,4,128]{2,1,0:T(4,128)S(1)}, f32[32,4,128]{2,1,0:T(4,128)S(1)}, u32[]{:S(2)}, u32[]{:S(2)}) collective-permute-start(f32[32,4,128]{2,1,0:T(4,128)S(1)} %get-tuple-element.258), channel_id=1, source_target_pairs={{2,0},{3,1},{6,4},{7,5},{10,8},{11,9},{14,12},{15,13},{18,16},{19,... | collective-permute-start | bytes 196616 | tf_op jit(solution)/shard_map/ppermute | solution.py:27
  80.3 6.2 %collective-permute-start.13 = (f32[32,4,128]{2,1,0:T(4,128)S(1)}, f32[32,4,128]{2,1,0:T(4,128)S(1)}, u32[]{:S(2)}, u32[]{:S(2)}) collective-permute-start(f32[32,4,128]{2,1,0:T(4,128)S(1)} %get-tuple-element.256), channel_id=1, source_target_pairs={{2,0},{3,1},{6,4},{7,5},{10,8},{11,9},{14,12},{15,13},{18,16},{19,... | collective-permute-start | bytes 196616 | tf_op jit(solution)/shard_map/ppermute | solution.py:27
  94.4 6.2 %collective-permute-start.17 = (f32[32,4,128]{2,1,0:T(4,128)S(1)}, f32[32,4,128]{2,1,0:T(4,128)S(1)}, u32[]{:S(2)}, u32[]{:S(2)}) collective-permute-start(f32[32,4,128]{2,1,0:T(4,128)S(1)} %get-tuple-element.254), channel_id=1, source_target_pairs={{2,0},{3,1},{6,4},{7,5},{10,8},{11,9},{14,12},{15,13},{18,16},{19,... | collective-permute-start | bytes 196616 | tf_op jit(solution)/shard_map/ppermute | solution.py:27
  113.0 6.2 %collective-permute-start.21 = (f32[32,4,128]{2,1,0:T(4,128)S(1)}, f32[32,4,128]{2,1,0:T(4,128)S(1)}, u32[]{:S(2)}, u32[]{:S(2)}) collective-permute-start(f32[32,4,128]{2,1,0:T(4,128)S(1)} %get-tuple-element.248), channel_id=1, source_target_pairs={{2,0},{3,1},{6,4},{7,5},{10,8},{11,9},{14,12},{15,13},{18,16},{19,... | collective-permute-start | bytes 196616 | tf_op jit(solution)/shard_map/ppermute | solution.py:27
  127.4 6.8 %collective-permute-start.25 = (f32[32,4,128]{2,1,0:T(4,128)S(1)}, f32[32,4,128]{2,1,0:T(4,128)S(1)}, u32[]{:S(2)}, u32[]{:S(2)}) collective-permute-start(f32[32,4,128]{2,1,0:T(4,128)S(1)} %get-tuple-element.246), channel_id=1, source_target_pairs={{2,0},{3,1},{6,4},{7,5},{10,8},{11,9},{14,12},{15,13},{18,16},{19,... | collective-permute-start | bytes 196616 | tf_op jit(solution)/shard_map/ppermute | solution.py:27
  134.4 7.9 %collective-permute-start.26 = (f32[32,16,4]{2,1,0:T(8,128)S(1)}, f32[32,16,4]{2,1,0:T(8,128)S(1)}, u32[]{:S(2)}, u32[]{:S(2)}) collective-permute-start(f32[32,16,4]{2,1,0:T(8,128)S(1)} %get-tuple-element.213), channel_id=1, source_target_pairs={{0,1},{2,3},{4,5},{6,7},{8,9},{10,11},{12,13},{14,15},{16,17},{18,... | collective-permute-start | bytes 24584 | tf_op jit(solution)/shard_map/ppermute | solution.py:25
  136.4 6.0 %collective-permute-start.27 = (f32[32,16,4]{2,1,0:T(8,128)S(1)}, f32[32,16,4]{2,1,0:T(8,128)S(1)}, u32[]{:S(2)}, u32[]{:S(2)}) collective-permute-start(f32[32,16,4]{2,1,0:T(8,128)S(1)} %get-tuple-element.212), channel_id=1, source_target_pairs={{1,0},{3,2},{5,4},{7,6},{9,8},{11,10},{13,12},{15,14},{17,16},{19,... | collective-permute-start | bytes 24584 | tf_op jit(solution)/shard_map/ppermute | solution.py:27
  143.8 8.7 %collective-permute-start.28 = (f32[32,4,128]{2,1,0:T(4,128)S(1)}, f32[32,4,128]{2,1,0:T(4,128)S(1)}, u32[]{:S(2)}, u32[]{:S(2)}) collective-permute-start(f32[32,4,128]{2,1,0:T(4,128)S(1)} %get-tuple-element.245), channel_id=1, source_target_pairs={{0,2},{1,3},{4,6},{5,7},{8,10},{9,11},{12,14},{13,15},{16,18},{17,... | collective-permute-start | bytes 196616 | tf_op jit(solution)/shard_map/ppermute | solution.py:25
  145.3 7.2 %collective-permute-start.29 = (f32[32,4,128]{2,1,0:T(4,128)S(1)}, f32[32,4,128]{2,1,0:T(4,128)S(1)}, u32[]{:S(2)}, u32[]{:S(2)}) collective-permute-start(f32[32,4,128]{2,1,0:T(4,128)S(1)} %get-tuple-element.244), channel_id=1, source_target_pairs={{2,0},{3,1},{6,4},{7,5},{10,8},{11,9},{14,12},{15,13},{18,16},{19,... | collective-permute-start | bytes 196616 | tf_op jit(solution)/shard_map/ppermute | solution.py:27
  146.6 9.9 %collective-permute-start.32 = (f32[32,4,128]{2,1,0:T(4,128)S(1)}, f32[32,4,128]{2,1,0:T(4,128)S(1)}, u32[]{:S(2)}, u32[]{:S(2)}) collective-permute-start(f32[32,4,128]{2,1,0:T(4,128)S(1)} %get-tuple-element.253), channel_id=1, source_target_pairs={{0,2},{1,3},{4,6},{5,7},{8,10},{9,11},{12,14},{13,15},{16,18},{17,... | collective-permute-start | bytes 196616 | tf_op jit(solution)/shard_map/ppermute | solution.py:25
  151.2 6.3 %collective-permute-start.33 = (f32[32,4,128]{2,1,0:T(4,128)S(1)}, f32[32,4,128]{2,1,0:T(4,128)S(1)}, u32[]{:S(2)}, u32[]{:S(2)}) collective-permute-start(f32[32,4,128]{2,1,0:T(4,128)S(1)} %get-tuple-element.252), channel_id=1, source_target_pairs={{2,0},{3,1},{6,4},{7,5},{10,8},{11,9},{14,12},{15,13},{18,16},{19,... | collective-permute-start | bytes 196616 | tf_op jit(solution)/shard_map/ppermute | solution.py:27
  160.8 5.9 %collective-permute-start.34 = (f32[32,16,4]{2,1,0:T(8,128)S(1)}, f32[32,16,4]{2,1,0:T(8,128)S(1)}, u32[]{:S(2)}, u32[]{:S(2)}) collective-permute-start(f32[32,16,4]{2,1,0:T(8,128)S(1)} %get-tuple-element.225), channel_id=1, source_target_pairs={{0,1},{2,3},{4,5},{6,7},{8,9},{10,11},{12,13},{14,15},{16,17},{18,... | collective-permute-start | bytes 24584 | tf_op jit(solution)/shard_map/ppermute | solution.py:25
  208.1 7.6 %collective-permute-start.36 = (f32[32,4,128]{2,1,0:T(4,128)S(1)}, f32[32,4,128]{2,1,0:T(4,128)S(1)}, u32[]{:S(2)}, u32[]{:S(2)}) collective-permute-start(f32[32,4,128]{2,1,0:T(4,128)S(1)} %get-tuple-element.243), channel_id=1, source_target_pairs={{0,2},{1,3},{4,6},{5,7},{8,10},{9,11},{12,14},{13,15},{16,18},{17,... | collective-permute-start | bytes 196616 | tf_op jit(solution)/shard_map/ppermute | solution.py:25
  211.8 6.2 %collective-permute-start.37 = (f32[32,4,128]{2,1,0:T(4,128)S(1)}, f32[32,4,128]{2,1,0:T(4,128)S(1)}, u32[]{:S(2)}, u32[]{:S(2)}) collective-permute-start(f32[32,4,128]{2,1,0:T(4,128)S(1)} %get-tuple-element.242), channel_id=1, source_target_pairs={{2,0},{3,1},{6,4},{7,5},{10,8},{11,9},{14,12},{15,13},{18,16},{19,... | collective-permute-start | bytes 196616 | tf_op jit(solution)/shard_map/ppermute | solution.py:27
  (28 other events, 109.3 us)
Sparse Core Ops, SparseCore 0:
  160.8 37.5 all-reduce.12
where the time goes:
time: 233 us; the launch traced here: 232 us
  starting transfers between devices  74 us (32%)
  waiting for transfers between devices  63 us (27%)
  other arithmetic  45.3 us (19%)
  blocking collectives  19.9 us (9%)
  between operations  19.5 us (8%)
  local copies, waits for them, and re-layouts  10.1 us (4%)
    ppermute x20, starting transfers between devices, padded_2(): lax.ppermute(tail, axis, [(i, (i + 1) % count) for i in range(ends)])  47.7 us
    psum x1, waiting for transfers between devices, shards(): grad_all, illum_all = lax.psum((grad, illum), 'shots')  31.3 us
    ppermute x20, waiting for transfers between devices, padded_2(): lax.ppermute(head, axis, [((i + 1) % count, i) for i in range(ends)])  29.7 us
    ppermute x20, starting transfers between devices, padded_2(): lax.ppermute(head, axis, [((i + 1) % count, i) for i in range(ends)])  26.2 us
    scatter-add x10, other arithmetic, place_local(): flat = jnp.zeros((rows * cols,), jnp.float32).at[spots].add(kept)  24.9 us
    all_gather x1, blocking collectives, shards(): full_vel = lax.all_gather(velocity, 'shots', axis=0, tiled=True)  13.6 us
    concatenate x30, other arithmetic, padded_2(): jnp.concatenate([lax.ppermute(tail, axis, [(i, (i + 1) % count) for i in...  8.09 us
    pmax x1, blocking collectives, shards(): peak = lax.pmax(jnp.max(jnp.abs(precond)), ('dom', 'sub'))  6.3 us
  transfers between devices with their start and end apart: 41, of which 16 were waited for; matrix products, arithmetic and copies ran while one was open for 14% of the time, Pallas kernels for 0%

commit v1 on v0

--- a/solution.py
+++ b/solution.py
@@ -75,7 +75,26 @@
     velocity, wave_prev, wave_now, adj_next, adj_now, sponge, wavelet, src_pos, rec_pos, observed
 ):
     depth, rows, cols = sponge.shape
-    full_vel = lax.all_gather(velocity, "shots", axis=0, tiled=True)
+    peers, position, rows_2 = (lax.axis_size("shots"), lax.axis_index("shots"), velocity.shape[0])
+    right = [(i_2, (i_2 + 1) % peers) for i_2 in range(peers)]
+    left = [(i_2, (i_2 - 1) % peers) for i_2 in range(peers)]
+    filled = jnp.zeros(
+        (*velocity.shape[:0], peers * rows_2, *velocity.shape[0 + 1 :]), velocity.dtype
+    )
+    filled = lax.dynamic_update_slice_in_dim(filled, velocity, position * rows_2, axis=0)
+    from_left = from_right = velocity
+    halfway = peers // 2
+    for hop in range(1, halfway + 1):
+        from_left = lax.ppermute(from_left, "shots", right)
+        filled = lax.dynamic_update_slice_in_dim(
+            filled, from_left, (position - hop) % peers * rows_2, axis=0
+        )
+        if hop < peers - halfway:
+            from_right = lax.ppermute(from_right, "shots", left)
+            filled = lax.dynamic_update_slice_in_dim(
+                filled, from_right, (position + hop) % peers * rows_2, axis=0
+            )
+    full_vel = filled
     kappa = full_vel * full_vel
     damp = damp_rate * sponge.astype(jnp.float32)
     amps = wavelet[0]

time: 233 us -> 225 us (0.966)
  blocking collectives: 19.9 us -> 6.3 us
  starting transfers between devices: 74 us -> 77.7 us
    all_gather x1 -> x0, blocking collectives: 13.6 us -> none  [shards(): full_vel = lax.all_gather(velocity, 'shots', axis=0, tiled=True)]
    ppermute x0 -> x3, starting transfers between devices: none -> 5.26 us  [the longest x2 3.16 us: shards(): from_left = lax.ppermute(from_left, 'shots', right)]
  transfers between devices with their start and end apart: 41 -> 44, of which waited for: 16 -> 17; matrix products, arithmetic and copies ran while one was open for 14% -> 15% of each run, Pallas kernels for 0% -> 0%
where the time goes in v1:
time: 225 us; the launch traced here: 224 us
  starting transfers between devices  77.7 us (35%)
  waiting for transfers between devices  63.5 us (28%)
  other arithmetic  45.6 us (20%)
  between operations  19.7 us (9%)
  local copies, waits for them, and re-layouts  10.9 us (5%)
  blocking collectives  6.3 us (3%)
    ppermute x20, starting transfers between devices, padded_2(): lax.ppermute(tail, axis, [(i, (i + 1) % count) for i in range(ends)])  46.2 us
    psum x1, waiting for transfers between devices, shards(): grad_all, illum_all = lax.psum((grad, illum), 'shots')  31.6 us
    ppermute x20, waiting for transfers between devices, padded_2(): lax.ppermute(head, axis, [((i + 1) % count, i) for i in range(ends)])  30 us
    ppermute x20, starting transfers between devices, padded_2(): lax.ppermute(head, axis, [((i + 1) % count, i) for i in range(ends)])  26.2 us
    scatter-add x10, other arithmetic, place_local(): flat = jnp.zeros((rows * cols,), jnp.float32).at[spots].add(kept)  25.2 us
    concatenate x30, other arithmetic, padded_2(): jnp.concatenate([lax.ppermute(tail, axis, [(i, (i + 1) % count) for i in...  8.1 us
    pmax x1, blocking collectives, shards(): peak = lax.pmax(jnp.max(jnp.abs(precond)), ('dom', 'sub'))  6.3 us
    add x10, other arithmetic, advance(): numer = 2.0 * now - (1.0 - damp) * before + kappa * lap  6.14 us
  transfers between devices with their start and end apart: 44, of which 17 were waited for; matrix products, arithmetic and copies ran while one was open for 15% of the time, Pallas kernels for 0%

profile of v1, /device:TPU:0, one launch (start us, length us, event | category | flops | bytes accessed | tf_op | source)
XLA Modules:
  0.0 223.8 jit_solution(8044189894516013778)
XLA Ops:
  7.2 3.1 %collective-permute-start = (f32[8,8,128]{2,1,0:T(8,128)}, f32[8,8,128]{2,1,0:T(8,128)S(1)}, u32[]{:S(2)}, u32[]{:S(2)}) collective-permute-start(f32[8,8,128]{2,1,0:T(8,128)} %param.42), channel_id=1, source_target_pairs={{0,4},{4,8},{8,12},{12,0},{1,5},{5,9},{9,13},{13,1},{2,6},{6,10},{... | collective-permute-start | bytes 98312 | tf_op jit(solution)/shard_map/ppermute | solution.py:88
  13.3 3.6 %collective-permute-start.7 = (f32[32,4,128]{2,1,0:T(4,128)S(1)}, f32[32,4,128]{2,1,0:T(4,128)S(1)}, u32[]{:S(2)}, u32[]{:S(2)}) collective-permute-start(f32[32,4,128]{2,1,0:T(4,128)S(1)} %get-tuple-element.261), channel_id=1, source_target_pairs={{0,2},{1,3},{4,6},{5,7},{8,10},{9,11},{12,14},{13,15},{16,18},{17,... | collective-permute-start | bytes 196616 | tf_op jit(solution)/shard_map/ppermute | solution.py:25
  18.2 4.5 %collective-permute-start.3 = (f32[32,4,128]{2,1,0:T(4,128)S(1)}, f32[32,4,128]{2,1,0:T(4,128)S(1)}, u32[]{:S(2)}, u32[]{:S(2)}) collective-permute-start(f32[32,4,128]{2,1,0:T(4,128)S(1)} %get-tuple-element.251), channel_id=1, source_target_pairs={{0,2},{1,3},{4,6},{5,7},{8,10},{9,11},{12,14},{13,15},{16,18},{17,... | collective-permute-start | bytes 196616 | tf_op jit(solution)/shard_map/ppermute | solution.py:25
  30.6 2.7 %fusion.344 = f32[1024]{0:T(1024)S(1)} fusion(f32[1024]{0:T(1024)S(1)} %broadcast.402.clone, s32[]{:T(128)} %bitcast.12, pred[1]{0:T(512)(128)(4,1)} %get-tuple-element.275, f32[1,1]{1,0:T(1,128)} %get-tuple-element.270, s32[1]{0:T(128)} %compare_select_fusion.1), kind=kLoop, calls=%fused_computation.689 | loop fusion | flops 5 | bytes 525 | tf_op jit(solution)/shard_map/scatter-add | solution.py:70
  33.3 2.6 %fusion.342 = f32[1024]{0:T(1024)S(1)} fusion(f32[1024]{0:T(1024)S(1)} %broadcast.402.clone.1, s32[]{:T(128)} %bitcast.12, pred[1]{0:T(512)(128)(4,1)} %get-tuple-element.275, f32[1,1]{1,0:T(1,128)} %get-tuple-element.269, s32[1]{0:T(128)} %compare_select_fusion.1), kind=kLoop, calls=%fused_computation.686 | loop fusion | flops 5 | bytes 525 | tf_op jit(solution)/shard_map/scatter-add | solution.py:70
  35.9 2.7 %fusion.340 = f32[1024]{0:T(1024)S(1)} fusion(f32[1024]{0:T(1024)S(1)} %broadcast.402.clone.2, s32[]{:T(128)} %bitcast.12, pred[1]{0:T(512)(128)(4,1)} %get-tuple-element.275, f32[1,1]{1,0:T(1,128)} %get-tuple-element.268, s32[1]{0:T(128)} %compare_select_fusion.1), kind=kLoop, calls=%fused_computation.683 | loop fusion | flops 5 | bytes 525 | tf_op jit(solution)/shard_map/scatter-add | solution.py:70
  38.6 2.6 %fusion.338 = f32[1024]{0:T(1024)S(1)} fusion(f32[1024]{0:T(1024)S(1)} %broadcast.402.clone.3, s32[]{:T(128)} %bitcast.12, pred[1]{0:T(512)(128)(4,1)} %get-tuple-element.275, f32[1,1]{1,0:T(1,128)} %get-tuple-element.267, s32[1]{0:T(128)} %compare_select_fusion.1), kind=kLoop, calls=%fused_computation.680 | loop fusion | flops 5 | bytes 525 | tf_op jit(solution)/shard_map/scatter-add | solution.py:70
  44.2 3.1 %collective-permute-start.9 = (f32[32,16,4]{2,1,0:T(8,128)S(1)}, f32[32,16,4]{2,1,0:T(8,128)S(1)}, u32[]{:S(2)}, u32[]{:S(2)}) collective-permute-start(f32[32,16,4]{2,1,0:T(8,128)S(1)} %get-tuple-element.241), channel_id=1, source_target_pairs={{0,1},{2,3},{4,5},{6,7},{8,9},{10,11},{12,13},{14,15},{16,17},{18,... | collective-permute-start | bytes 24584 | tf_op jit(solution)/shard_map/ppermute | solution.py:25
  52.2 4.4 %collective-permute-start.11 = (f32[32,4,128]{2,1,0:T(4,128)S(1)}, f32[32,4,128]{2,1,0:T(4,128)S(1)}, u32[]{:S(2)}, u32[]{:S(2)}) collective-permute-start(f32[32,4,128]{2,1,0:T(4,128)S(1)} %get-tuple-element.259), channel_id=1, source_target_pairs={{0,2},{1,3},{4,6},{5,7},{8,10},{9,11},{12,14},{13,15},{16,18},{17,... | collective-permute-start | bytes 196616 | tf_op jit(solution)/shard_map/ppermute | solution.py:25
  58.9 4.5 %collective-permute-done.12 = f32[32,4,128]{2,1,0:T(4,128)S(1)} collective-permute-done((f32[32,4,128]{2,1,0:T(4,128)S(1)}, f32[32,4,128]{2,1,0:T(4,128)S(1)}, u32[]{:S(2)}, u32[]{:S(2)}) %collective-permute-start.12) | collective-permute-done | bytes 65568 | tf_op jit(solution)/shard_map/ppermute | solution.py:27
  74.6 3.5 %collective-permute-done.16 = f32[32,4,128]{2,1,0:T(4,128)S(1)} collective-permute-done((f32[32,4,128]{2,1,0:T(4,128)S(1)}, f32[32,4,128]{2,1,0:T(4,128)S(1)}, u32[]{:S(2)}, u32[]{:S(2)}) %collective-permute-start.16) | collective-permute-done | bytes 65568 | tf_op jit(solution)/shard_map/ppermute | solution.py:27
  88.7 3.5 %collective-permute-done.20 = f32[32,4,128]{2,1,0:T(4,128)S(1)} collective-permute-done((f32[32,4,128]{2,1,0:T(4,128)S(1)}, f32[32,4,128]{2,1,0:T(4,128)S(1)}, u32[]{:S(2)}, u32[]{:S(2)}) %collective-permute-start.20) | collective-permute-done | bytes 65568 | tf_op jit(solution)/shard_map/ppermute | solution.py:27
  100.6 2.3 %scatter_custom_fusion = f32[1024]{0:T(1024)S(1)} fusion(s32[256]{0:T(256)S(1)} %bitcast.109, f32[256]{0:T(256)S(1)} %get-tuple-element.274, f32[]{:T(128)} %constant.427.clone.1), kind=kCustom, calls=%fused_computation.650 | custom fusion | flops 256 | bytes 4100 | tf_op jit(solution)/shard_map/scatter-add | solution.py:70
  106.7 4.1 %collective-permute-done.24 = f32[32,4,128]{2,1,0:T(4,128)S(1)} collective-permute-done((f32[32,4,128]{2,1,0:T(4,128)S(1)}, f32[32,4,128]{2,1,0:T(4,128)S(1)}, u32[]{:S(2)}, u32[]{:S(2)}) %collective-permute-start.24) | collective-permute-done | bytes 65568 | tf_op jit(solution)/shard_map/ppermute | solution.py:27
  113.7 2.3 %scatter_custom_fusion.1 = f32[1024]{0:T(1024)S(1)} fusion(s32[256]{0:T(256)S(1)} %bitcast.110, f32[256]{0:T(256)S(1)} %get-tuple-element.273, f32[]{:T(128)} %constant.427.clone.1), kind=kCustom, calls=%fused_computation.648 | custom fusion | flops 256 | bytes 4100 | tf_op jit(solution)/shard_map/scatter-add | solution.py:70
  121.3 4.5 %collective-permute-done.28 = f32[32,4,128]{2,1,0:T(4,128)S(1)} collective-permute-done((f32[32,4,128]{2,1,0:T(4,128)S(1)}, f32[32,4,128]{2,1,0:T(4,128)S(1)}, u32[]{:S(2)}, u32[]{:S(2)}) %collective-permute-start.28) | collective-permute-done | bytes 65568 | tf_op jit(solution)/shard_map/ppermute | solution.py:27
  129.3 2.3 %scatter_custom_fusion.3 = f32[1024]{0:T(1024)S(1)} fusion(s32[256]{0:T(256)S(1)} %bitcast.111, f32[256]{0:T(256)S(1)} %get-tuple-element.200, f32[]{:T(128)} %constant.427.clone.1), kind=kCustom, calls=%fused_computation.644 | custom fusion | flops 256 | bytes 4100 | tf_op jit(solution)/shard_map/scatter-add | solution.py:70
  138.2 4.5 %collective-permute-start.35 = (f32[32,4,128]{2,1,0:T(4,128)S(1)}, f32[32,4,128]{2,1,0:T(4,128)S(1)}, u32[]{:S(2)}, u32[]{:S(2)}) collective-permute-start(f32[32,4,128]{2,1,0:T(4,128)S(1)} %get-tuple-element.253), channel_id=1, source_target_pairs={{0,2},{1,3},{4,6},{5,7},{8,10},{9,11},{12,14},{13,15},{16,18},{17,... | collective-permute-start | bytes 196616 | tf_op jit(solution)/shard_map/ppermute | solution.py:25
  144.3 2.3 %collective-permute-start.33 = (f32[32,16,4]{2,1,0:T(8,128)S(1)}, f32[32,16,4]{2,1,0:T(8,128)S(1)}, u32[]{:S(2)}, u32[]{:S(2)}) collective-permute-start(f32[32,16,4]{2,1,0:T(8,128)S(1)} %get-tuple-element.209), channel_id=1, source_target_pairs={{0,1},{2,3},{4,5},{6,7},{8,9},{10,11},{12,13},{14,15},{16,17},{18,... | collective-permute-start | bytes 24584 | tf_op jit(solution)/shard_map/ppermute | solution.py:25
  155.8 2.7 %fusion.336 = f32[1024]{0:T(1024)S(1)} fusion(f32[1024]{0:T(1024)S(1)} %broadcast.402.clone.4, s32[]{:T(128)} %bitcast.12, pred[1]{0:T(512)(128)(4,1)} %get-tuple-element.275, f32[1,1]{1,0:T(1,128)} %get-tuple-element.271, s32[1]{0:T(128)} %compare_select_fusion.1), kind=kLoop, calls=%fused_computation.677 | loop fusion | flops 5 | bytes 525 | tf_op jit(solution)/shard_map/scatter-add | solution.py:70
  158.8 31.6 %all-reduce.13.cloned.1.call-done = (f32[32,8,128]{2,1,0:T(8,128)}, f32[32,8,128]{2,1,0:T(8,128)}) async-done(((f32[32,8,128]{2,1,0:T(8,128)}, f32[32,8,128]{2,1,0:T(8,128)}), (f32[32,8,128]{2,1,0:T(8,128)}, f32[32,8,128]{2,1,0:T(8,128)})) %all-reduce.13.cloned.1.call-update) | async-done | bytes 262160 | tf_op jit(solution)/shard_map/psum | solution.py:123
  192.4 6.3 %pmax.7 = f32[]{:T(128)} all-reduce(f32[]{:T(128)} %abs_reduce_fusion), channel_id=1, replica_groups=mesh['groups'=2,'shots'=4,'dom'=2,'sub'=2] {'dom','sub'}, use_global_device_ids=true, to_apply=%region_7.8 | all-reduce | flops 1 | bytes 8 | tf_op jit(solution)/shard_map/pmax | solution.py:125
  200.1 3.6 %collective-permute-start.39 = (f32[32,4,128]{2,1,0:T(4,128)S(1)}, f32[32,4,128]{2,1,0:T(4,128)S(1)}, u32[]{:S(2)}, u32[]{:S(2)}) collective-permute-start(f32[32,4,128]{2,1,0:T(4,128)S(1)} %get-tuple-element.243), channel_id=1, source_target_pairs={{0,2},{1,3},{4,6},{5,7},{8,10},{9,11},{12,14},{13,15},{16,18},{17,... | collective-permute-start | bytes 196616 | tf_op jit(solution)/shard_map/ppermute | solution.py:25
  205.1 2.6 %fusion.334 = f32[1024]{0:T(1024)S(1)} fusion(f32[1024]{0:T(1024)S(1)} %broadcast.402.clone.5, s32[]{:T(128)} %bitcast.12, pred[1]{0:T(512)(128)(4,1)} %get-tuple-element.275, f32[1,1]{1,0:T(1,128)} %get-tuple-element.266, s32[1]{0:T(128)} %compare_select_fusion.1), kind=kLoop, calls=%fused_computation.674 | loop fusion | flops 5 | bytes 525 | tf_op jit(solution)/shard_map/scatter-add | solution.py:70
  (208 shorter events, 94.2 us)
Async XLA Ops:
  7.2 183.2 %all-reduce.13.cloned.1.call-start = ((), (), s32[]{:S(2)}) async-start(), calls=%async_computation | async-start | bytes 524288 | tf_op jit(solution)/shard_map/psum | solution.py:123
  7.2 34.0 %collective-permute-start = (f32[8,8,128]{2,1,0:T(8,128)}, f32[8,8,128]{2,1,0:T(8,128)S(1)}, u32[]{:S(2)}, u32[]{:S(2)}) collective-permute-start(f32[8,8,128]{2,1,0:T(8,128)} %param.42), channel_id=1, source_target_pairs={{0,4},{4,8},{8,12},{12,0},{1,5},{5,9},{9,13},{13,1},{2,6},{6,10},{... | collective-permute-start | bytes 98312 | tf_op jit(solution)/shard_map/ppermute | solution.py:88
  10.3 32.2 %collective-permute-start.1 = (f32[8,8,128]{2,1,0:T(8,128)}, f32[8,8,128]{2,1,0:T(8,128)S(1)}, u32[]{:S(2)}, u32[]{:S(2)}) collective-permute-start(f32[8,8,128]{2,1,0:T(8,128)} %param.42), channel_id=1, source_target_pairs={{0,12},{4,0},{8,4},{12,8},{1,13},{5,1},{9,5},{13,9},{2,14},{6,2},{... | collective-permute-start | bytes 98312 | tf_op jit(solution)/shard_map/ppermute | solution.py:93
  13.3 29.3 %collective-permute-start.7 = (f32[32,4,128]{2,1,0:T(4,128)S(1)}, f32[32,4,128]{2,1,0:T(4,128)S(1)}, u32[]{:S(2)}, u32[]{:S(2)}) collective-permute-start(f32[32,4,128]{2,1,0:T(4,128)S(1)} %get-tuple-element.261), channel_id=1, source_target_pairs={{0,2},{1,3},{4,6},{5,7},{8,10},{9,11},{12,14},{13,15},{16,18},{17,... | collective-permute-start | bytes 196616 | tf_op jit(solution)/shard_map/ppermute | solution.py:25
  16.9 25.8 %collective-permute-start.8 = (f32[32,4,128]{2,1,0:T(4,128)S(1)}, f32[32,4,128]{2,1,0:T(4,128)S(1)}, u32[]{:S(2)}, u32[]{:S(2)}) collective-permute-start(f32[32,4,128]{2,1,0:T(4,128)S(1)} %get-tuple-element.260), channel_id=1, source_target_pairs={{2,0},{3,1},{6,4},{7,5},{10,8},{11,9},{14,12},{15,13},{18,16},{19,... | collective-permute-start | bytes 196616 | tf_op jit(solution)/shard_map/ppermute | solution.py:27
  18.2 29.0 %collective-permute-start.3 = (f32[32,4,128]{2,1,0:T(4,128)S(1)}, f32[32,4,128]{2,1,0:T(4,128)S(1)}, u32[]{:S(2)}, u32[]{:S(2)}) collective-permute-start(f32[32,4,128]{2,1,0:T(4,128)S(1)} %get-tuple-element.251), channel_id=1, source_target_pairs={{0,2},{1,3},{4,6},{5,7},{8,10},{9,11},{12,14},{13,15},{16,18},{17,... | collective-permute-start | bytes 196616 | tf_op jit(solution)/shard_map/ppermute | solution.py:25
  41.2 6.1 %collective-permute-start.4 = (f32[32,4,128]{2,1,0:T(4,128)S(1)}, f32[32,4,128]{2,1,0:T(4,128)S(1)}, u32[]{:S(2)}, u32[]{:S(2)}) collective-permute-start(f32[32,4,128]{2,1,0:T(4,128)S(1)} %get-tuple-element.250), channel_id=1, source_target_pairs={{2,0},{3,1},{6,4},{7,5},{10,8},{11,9},{14,12},{15,13},{18,16},{19,... | collective-permute-start | bytes 196616 | tf_op jit(solution)/shard_map/ppermute | solution.py:27
  42.6 7.6 %collective-permute-start.2 = (f32[8,8,128]{2,1,0:T(8,128)S(1)}, f32[8,8,128]{2,1,0:T(8,128)S(1)}, u32[]{:S(2)}, u32[]{:S(2)}) collective-permute-start(f32[8,8,128]{2,1,0:T(8,128)S(1)} %collective-permute-done), channel_id=1, source_target_pairs={{0,4},{4,8},{8,12},{12,0},{1,5},{5,9},{9,13},{13,1},{2,6},{6,10},{... | collective-permute-start | bytes 98312 | tf_op jit(solution)/shard_map/ppermute | solution.py:88
  42.9 7.4 %collective-permute-start.10 = (f32[32,16,4]{2,1,0:T(8,128)S(1)}, f32[32,16,4]{2,1,0:T(8,128)S(1)}, u32[]{:S(2)}, u32[]{:S(2)}) collective-permute-start(f32[32,16,4]{2,1,0:T(8,128)S(1)} %get-tuple-element.240), channel_id=1, source_target_pairs={{1,0},{3,2},{5,4},{7,6},{9,8},{11,10},{13,12},{15,14},{17,16},{19,... | collective-permute-start | bytes 24584 | tf_op jit(solution)/shard_map/ppermute | solution.py:27
  47.6 10.4 %collective-permute-start.5 = (f32[32,16,4]{2,1,0:T(8,128)S(1)}, f32[32,16,4]{2,1,0:T(8,128)S(1)}, u32[]{:S(2)}, u32[]{:S(2)}) collective-permute-start(f32[32,16,4]{2,1,0:T(8,128)S(1)} %get-tuple-element.221), channel_id=1, source_target_pairs={{0,1},{2,3},{4,5},{6,7},{8,9},{10,11},{12,13},{14,15},{16,17},{18,... | collective-permute-start | bytes 24584 | tf_op jit(solution)/shard_map/ppermute | solution.py:25
  48.9 9.1 %collective-permute-start.6 = (f32[32,16,4]{2,1,0:T(8,128)S(1)}, f32[32,16,4]{2,1,0:T(8,128)S(1)}, u32[]{:S(2)}, u32[]{:S(2)}) collective-permute-start(f32[32,16,4]{2,1,0:T(8,128)S(1)} %get-tuple-element.220), channel_id=1, source_target_pairs={{1,0},{3,2},{5,4},{7,6},{9,8},{11,10},{13,12},{15,14},{17,16},{19,... | collective-permute-start | bytes 24584 | tf_op jit(solution)/shard_map/ppermute | solution.py:27
  52.2 6.7 %collective-permute-start.11 = (f32[32,4,128]{2,1,0:T(4,128)S(1)}, f32[32,4,128]{2,1,0:T(4,128)S(1)}, u32[]{:S(2)}, u32[]{:S(2)}) collective-permute-start(f32[32,4,128]{2,1,0:T(4,128)S(1)} %get-tuple-element.259), channel_id=1, source_target_pairs={{0,2},{1,3},{4,6},{5,7},{8,10},{9,11},{12,14},{13,15},{16,18},{17,... | collective-permute-start | bytes 196616 | tf_op jit(solution)/shard_map/ppermute | solution.py:25
  56.6 6.7 %collective-permute-start.12 = (f32[32,4,128]{2,1,0:T(4,128)S(1)}, f32[32,4,128]{2,1,0:T(4,128)S(1)}, u32[]{:S(2)}, u32[]{:S(2)}) collective-permute-start(f32[32,4,128]{2,1,0:T(4,128)S(1)} %get-tuple-element.258), channel_id=1, source_target_pairs={{2,0},{3,1},{6,4},{7,5},{10,8},{11,9},{14,12},{15,13},{18,16},{19,... | collective-permute-start | bytes 196616 | tf_op jit(solution)/shard_map/ppermute | solution.py:27
  71.9 6.2 %collective-permute-start.16 = (f32[32,4,128]{2,1,0:T(4,128)S(1)}, f32[32,4,128]{2,1,0:T(4,128)S(1)}, u32[]{:S(2)}, u32[]{:S(2)}) collective-permute-start(f32[32,4,128]{2,1,0:T(4,128)S(1)} %get-tuple-element.256), channel_id=1, source_target_pairs={{2,0},{3,1},{6,4},{7,5},{10,8},{11,9},{14,12},{15,13},{18,16},{19,... | collective-permute-start | bytes 196616 | tf_op jit(solution)/shard_map/ppermute | solution.py:27
  86.0 6.2 %collective-permute-start.20 = (f32[32,4,128]{2,1,0:T(4,128)S(1)}, f32[32,4,128]{2,1,0:T(4,128)S(1)}, u32[]{:S(2)}, u32[]{:S(2)}) collective-permute-start(f32[32,4,128]{2,1,0:T(4,128)S(1)} %get-tuple-element.254), channel_id=1, source_target_pairs={{2,0},{3,1},{6,4},{7,5},{10,8},{11,9},{14,12},{15,13},{18,16},{19,... | collective-permute-start | bytes 196616 | tf_op jit(solution)/shard_map/ppermute | solution.py:27
  104.6 6.2 %collective-permute-start.24 = (f32[32,4,128]{2,1,0:T(4,128)S(1)}, f32[32,4,128]{2,1,0:T(4,128)S(1)}, u32[]{:S(2)}, u32[]{:S(2)}) collective-permute-start(f32[32,4,128]{2,1,0:T(4,128)S(1)} %get-tuple-element.248), channel_id=1, source_target_pairs={{2,0},{3,1},{6,4},{7,5},{10,8},{11,9},{14,12},{15,13},{18,16},{19,... | collective-permute-start | bytes 196616 | tf_op jit(solution)/shard_map/ppermute | solution.py:27
  119.0 6.8 %collective-permute-start.28 = (f32[32,4,128]{2,1,0:T(4,128)S(1)}, f32[32,4,128]{2,1,0:T(4,128)S(1)}, u32[]{:S(2)}, u32[]{:S(2)}) collective-permute-start(f32[32,4,128]{2,1,0:T(4,128)S(1)} %get-tuple-element.246), channel_id=1, source_target_pairs={{2,0},{3,1},{6,4},{7,5},{10,8},{11,9},{14,12},{15,13},{18,16},{19,... | collective-permute-start | bytes 196616 | tf_op jit(solution)/shard_map/ppermute | solution.py:27
  126.0 7.9 %collective-permute-start.29 = (f32[32,16,4]{2,1,0:T(8,128)S(1)}, f32[32,16,4]{2,1,0:T(8,128)S(1)}, u32[]{:S(2)}, u32[]{:S(2)}) collective-permute-start(f32[32,16,4]{2,1,0:T(8,128)S(1)} %get-tuple-element.213), channel_id=1, source_target_pairs={{0,1},{2,3},{4,5},{6,7},{8,9},{10,11},{12,13},{14,15},{16,17},{18,... | collective-permute-start | bytes 24584 | tf_op jit(solution)/shard_map/ppermute | solution.py:25
  135.4 8.7 %collective-permute-start.31 = (f32[32,4,128]{2,1,0:T(4,128)S(1)}, f32[32,4,128]{2,1,0:T(4,128)S(1)}, u32[]{:S(2)}, u32[]{:S(2)}) collective-permute-start(f32[32,4,128]{2,1,0:T(4,128)S(1)} %get-tuple-element.245), channel_id=1, source_target_pairs={{0,2},{1,3},{4,6},{5,7},{8,10},{9,11},{12,14},{13,15},{16,18},{17,... | collective-permute-start | bytes 196616 | tf_op jit(solution)/shard_map/ppermute | solution.py:25
  136.9 7.2 %collective-permute-start.32 = (f32[32,4,128]{2,1,0:T(4,128)S(1)}, f32[32,4,128]{2,1,0:T(4,128)S(1)}, u32[]{:S(2)}, u32[]{:S(2)}) collective-permute-start(f32[32,4,128]{2,1,0:T(4,128)S(1)} %get-tuple-element.244), channel_id=1, source_target_pairs={{2,0},{3,1},{6,4},{7,5},{10,8},{11,9},{14,12},{15,13},{18,16},{19,... | collective-permute-start | bytes 196616 | tf_op jit(solution)/shard_map/ppermute | solution.py:27
  138.2 9.9 %collective-permute-start.35 = (f32[32,4,128]{2,1,0:T(4,128)S(1)}, f32[32,4,128]{2,1,0:T(4,128)S(1)}, u32[]{:S(2)}, u32[]{:S(2)}) collective-permute-start(f32[32,4,128]{2,1,0:T(4,128)S(1)} %get-tuple-element.253), channel_id=1, source_target_pairs={{0,2},{1,3},{4,6},{5,7},{8,10},{9,11},{12,14},{13,15},{16,18},{17,... | collective-permute-start | bytes 196616 | tf_op jit(solution)/shard_map/ppermute | solution.py:25
  142.8 6.3 %collective-permute-start.36 = (f32[32,4,128]{2,1,0:T(4,128)S(1)}, f32[32,4,128]{2,1,0:T(4,128)S(1)}, u32[]{:S(2)}, u32[]{:S(2)}) collective-permute-start(f32[32,4,128]{2,1,0:T(4,128)S(1)} %get-tuple-element.252), channel_id=1, source_target_pairs={{2,0},{3,1},{6,4},{7,5},{10,8},{11,9},{14,12},{15,13},{18,16},{19,... | collective-permute-start | bytes 196616 | tf_op jit(solution)/shard_map/ppermute | solution.py:27
  200.1 7.5 %collective-permute-start.39 = (f32[32,4,128]{2,1,0:T(4,128)S(1)}, f32[32,4,128]{2,1,0:T(4,128)S(1)}, u32[]{:S(2)}, u32[]{:S(2)}) collective-permute-start(f32[32,4,128]{2,1,0:T(4,128)S(1)} %get-tuple-element.243), channel_id=1, source_target_pairs={{0,2},{1,3},{4,6},{5,7},{8,10},{9,11},{12,14},{13,15},{16,18},{17,... | collective-permute-start | bytes 196616 | tf_op jit(solution)/shard_map/ppermute | solution.py:25
  203.7 6.2 %collective-permute-start.40 = (f32[32,4,128]{2,1,0:T(4,128)S(1)}, f32[32,4,128]{2,1,0:T(4,128)S(1)}, u32[]{:S(2)}, u32[]{:S(2)}) collective-permute-start(f32[32,4,128]{2,1,0:T(4,128)S(1)} %get-tuple-element.242), channel_id=1, source_target_pairs={{2,0},{3,1},{6,4},{7,5},{10,8},{11,9},{14,12},{15,13},{18,16},{19,... | collective-permute-start | bytes 196616 | tf_op jit(solution)/shard_map/ppermute | solution.py:27
  (31 other events, 111.7 us)
Sparse Core Ops, SparseCore 0:
  152.4 37.9 all-reduce.12
